TPU v7x, 32 devices: a whole 2x2x4 slice. The times are simulated.
32 devices in a mesh: groups: 2 (over x), blk: 16 (over z, y, core).
Axes of the slice: x: 2, y: 2, z: 4, core: 2. Of those that a mesh axis runs over, the one named last changes fastest.
Arguments:
- frames: bfloat16 [256, 16384], P(('groups', 'blk')), parts along dimension 0
- basis: bfloat16 [256, 64], P(('groups', 'blk')), parts along dimension 0, may hold values from -6 to 6
- density: bfloat16 [256], P(('groups', 'blk')), parts along dimension 0, may hold values from 0.25 to 4
Outputs:
- residual_block: bfloat16 [256, 64], P(('groups', 'blk')), parts along dimension 0
- coefficients: float32 [128, 64], P('groups'), parts along dimension 0
There are 2 independent parts, one for each index of `groups`. A program takes and returns all parts, laid end to end along the dimension named above; each array names one. Nothing has to cross between parts.
All inputs are finite; a program needn't handle non-finite values.
Results may differ from a plain program's by a relative error of at most 0.0045.
Values may be sent and summed in bfloat16 or wider, within the bound.
No kernel may reach another device: no remote copies, remote signals or barrier semaphores. Data moves between devices by JAX's collectives and lax.ppermute only.
A program may use at most 64 MiB of HBM per device.

v0:
```python
import jax
import jax.numpy as jnp
from jax import lax
from jax.sharding import PartitionSpec as P


def pair_kernel(left, left_norms, right):
    right_norms = jnp.sum(jnp.square(right.astype(jnp.float32)), axis=1)
    inner_products = lax.dot_general(
        left, right, (((1,), (1,)), ((), ())), preferred_element_type=jnp.float32
    )
    squared_dist = left_norms[:, None] + right_norms[None, :] - 2.0 * inner_products
    return jnp.exp(-squared_dist / left.shape[1])


def shards(frames, basis, density):
    own_norms = jnp.sum(jnp.square(frames.astype(jnp.float32)), axis=1)
    row_count = frames.shape[0]
    blocks = lax.all_gather(frames, "blk", axis=0, tiled=True)
    vectors = lax.all_gather(basis, "blk", axis=0, tiled=True)
    weights_in = lax.all_gather(density, "blk", axis=0, tiled=True)
    kernel = pair_kernel(frames, own_norms, blocks)
    forward = (kernel * weights_in.astype(jnp.float32)[None, :]).astype(jnp.bfloat16)
    numer = jnp.dot(forward, vectors, preferred_element_type=jnp.float32)
    totals = jnp.sum(forward.astype(jnp.float32), axis=1)
    numer, totals = (numer, totals)
    applied = numer / totals[:, None]
    basis_f = basis.astype(jnp.float32)
    local_coef = lax.dot_general(
        basis_f,
        applied,
        (((0,), (0,)), ((), ())),
        precision=lax.Precision.HIGHEST,
        preferred_element_type=jnp.float32,
    )
    coefficients = lax.psum(local_coef, "blk")
    frame_total = row_count * lax.axis_size("blk")
    projection = jnp.dot(
        basis_f, coefficients, precision=lax.Precision.HIGHEST, preferred_element_type=jnp.float32
    )
    residual_block = (applied - projection / frame_total).astype(jnp.bfloat16)
    return (residual_block, coefficients)


def solution(mesh):
    placed = (P(("groups", "blk"), None), P(("groups", "blk"), None), P(("groups", "blk")))
    return jax.shard_map(
        shards,
        mesh=mesh,
        in_specs=placed,
        out_specs=(P(("groups", "blk"), None), P("groups", None)),
        check_vma=False,
    )
```

profile of v0, /device:TPU:0, one launch (start us, length us, event | category | flops | bytes accessed | tf_op | source)
XLA Modules:
  0.0 137.7 jit_solution(3754534518135585667)
XLA Ops:
  7.2 0.0 copy-start.1
  7.2 0.0 all-gather.2.cloned.1.call-start
  7.2 0.7 all-gather.2.cloned.1.call-update
  7.9 1.2 dynamic-slice
  9.8 0.9 dynamic-update-slice
  10.7 35.4 %all-reduce = bf16[128]{0:T(256)(128)(2,1)S(1)} all-reduce(bf16[128]{0:T(256)(128)(2,1)S(1)} %dynamic-update-slice), channel_id=1, replica_groups=mesh['groups'=2,'blk'=16] {'blk'}, use_global_device_ids=true, to_apply=%add | all-reduce | flops 128 | bytes 512
  46.1 17.6 %all_gather.11 = bf16[128,64]{1,0:T(8,128)(2,1)S(1)} all-gather(bf16[8,64]{1,0:T(8,128)(2,1)} %param.4), channel_id=1, replica_groups=mesh['groups'=2,'blk'=16] {'blk'}, dimensions={0}, use_global_device_ids=true | all-gather | bytes 17408 | tf_op jit(solution)/shard_map/all_gather | solution.py:20
  63.7 1.2 multiply_reduce_fusion.1
  64.9 0.0 all-gather.2.cloned.1.call-done
  64.9 0.0 copy-start
  64.9 0.0 copy-start.2
  64.9 3.2 %multiply_reduce_fusion = f32[128]{0:T(128)S(1)} fusion(bf16[128,16384]{1,0:T(8,128)(2,1)} %all-gather.2.cloned.1.call-done), kind=kLoop, calls=%fused_computation | loop fusion | flops 6291328 | bytes 4194816 | tf_op jit(solution)/shard_map/reduce_sum | solution.py:8
  68.2 0.0 copy-done.1
  68.2 0.2 copy-done
  68.4 1.3 convert_reduce_fusion
  69.7 0.1 convolution_divide_fusion
  69.8 0.0 copy-done.2
  69.8 0.2 convolution_bitcast_fusion
  70.0 59.3 %psum.7 = f32[64,64]{0,1:T(8,128)S(1)} all-reduce(f32[64,64]{0,1:T(8,128)S(1)} %convolution_bitcast_fusion), channel_id=1, replica_groups=mesh['groups'=2,'blk'=16] {'blk'}, use_global_device_ids=true, to_apply=%region_3.0 | all-reduce | flops 4096 | bytes 32768 | tf_op jit(solution)/shard_map/psum | solution.py:36
  129.4 0.7 fusion.8
  130.1 0.7 copy.5
  (2 shorter events, 0.0 us)
Async XLA Ops:
  7.2 61.0 %copy-start.1 = (bf16[8,16384]{1,0:T(8,128)(2,1)S(1)}, bf16[8,16384]{1,0:T(8,128)(2,1)}, u32[]{:S(2)}) copy-start(bf16[8,16384]{1,0:T(8,128)(2,1)} %param.3) | copy-start | bytes 786436
  7.2 57.7 %all-gather.2.cloned.1.call-start = ((), (), s32[]{:S(2)}) async-start(), calls=%async_computation | async-start | bytes 4456448 | tf_op jit(solution)/shard_map/all_gather | solution.py:19
  64.9 3.5 %copy-start = (bf16[128,16384]{1,0:T(8,128)(2,1)S(1)}, bf16[128,16384]{1,0:T(8,128)(2,1)}, u32[]{:S(2)}) copy-start(bf16[128,16384]{1,0:T(8,128)(2,1)} %all-gather.2.cloned.1.call-done) | copy-start | bytes 12582916
  64.9 4.9 %copy-start.2 = (bf16[8,64]{1,0:T(8,128)(2,1)S(1)}, bf16[8,64]{1,0:T(8,128)(2,1)}, u32[]{:S(2)}) copy-start(bf16[8,64]{1,0:T(8,128)(2,1)} %param.4) | copy-start | bytes 3076
Sparse Core Ops, SparseCore 0:
  10.2 53.5 all-gather.1
where the time goes:
time: 138 us
  blocking collectives  112 us (81%)
  between operations  14.7 us (11%)
  other arithmetic  4.43 us (3%)
  local copies, waits for them, and re-layouts  3.01 us (2%)
  matrix products  2.4 us (2%)
    psum x1, blocking collectives, shards(): coefficients = lax.psum(local_coef, 'blk')  59.3 us
    unnamed x1, blocking collectives  35.4 us
    all_gather x1, blocking collectives, shards(): vectors = lax.all_gather(basis, 'blk', axis=0, tiled=True)  17.6 us
    reduce_sum x1, other arithmetic, pair_kernel(): right_norms = jnp.sum(jnp.square(right.astype(jnp.float32)), axis=1)  3.23 us
    unnamed x10, local copies, waits for them, and re-layouts  3.01 us
  transfers between devices with their start and end apart: 1, of which 0 were waited for; matrix products, arithmetic and copies ran while one was open for 2% of the time, Pallas kernels for 0%

commit v1 on v0

--- a/solution.py
+++ b/solution.py
@@ -33,7 +33,11 @@
         precision=lax.Precision.HIGHEST,
         preferred_element_type=jnp.float32,
     )
-    coefficients = lax.psum(local_coef, "blk")
+    coefficients = local_coef
+    for hop in (1, 2, 4, 8):
+        coefficients = coefficients + lax.ppermute(
+            coefficients, "blk", [(dev, dev ^ hop) for dev in range(16)]
+        )
     frame_total = row_count * lax.axis_size("blk")
     projection = jnp.dot(
         basis_f, coefficients, precision=lax.Precision.HIGHEST, preferred_element_type=jnp.float32

time: 138 us -> 92.6 us (0.67)
  blocking collectives: 112 us -> 53 us
  waiting for transfers between devices: 0.69 us -> 11.3 us
  starting transfers between devices: 0.04 us -> 3.47 us
    psum x1 -> x0, blocking collectives: 59.3 us -> none  [shards(): coefficients = lax.psum(local_coef, 'blk')]
    ppermute x0 -> x4, waiting for transfers between devices: none -> 10.6 us  [shards(): lax.ppermute(coefficients, 'blk', [(dev, dev ^ hop) for dev in range(16)])]
    ppermute x0 -> x4, starting transfers between devices: none -> 3.43 us  [shards(): lax.ppermute(coefficients, 'blk', [(dev, dev ^ hop) for dev in range(16)])]
  transfers between devices with their start and end apart: 1 -> 5, of which waited for: 0 -> 4; matrix products, arithmetic and copies ran while one was open for 2% -> 4% of each run, Pallas kernels for 0% -> 0%
where the time goes in v1:
time: 92.6 us; the launch traced here: 92.4 us
  blocking collectives  53 us (57%)
  between operations  14.7 us (16%)
  waiting for transfers between devices  11.3 us (12%)
  other arithmetic  4.45 us (5%)
  starting transfers between devices  3.47 us (4%)
  local copies, waits for them, and re-layouts  3.01 us (3%)
  matrix products  2.4 us (3%)
    unnamed x1, blocking collectives  35.4 us
    all_gather x1, blocking collectives, shards(): vectors = lax.all_gather(basis, 'blk', axis=0, tiled=True)  17.6 us
    ppermute x4, waiting for transfers between devices, shards(): lax.ppermute(coefficients, 'blk', [(dev, dev ^ hop) for dev in range(16)])  10.6 us
    ppermute x4, starting transfers between devices, shards(): lax.ppermute(coefficients, 'blk', [(dev, dev ^ hop) for dev in range(16)])  3.43 us
    reduce_sum x1, other arithmetic, pair_kernel(): right_norms = jnp.sum(jnp.square(right.astype(jnp.float32)), axis=1)  3.23 us
    unnamed x10, local copies, waits for them, and re-layouts  3.01 us
  transfers between devices with their start and end apart: 5, of which 4 were waited for; matrix products, arithmetic and copies ran while one was open for 4% of the time, Pallas kernels for 0%

profile of v1, /device:TPU:0, one launch (start us, length us, event | category | flops | bytes accessed | tf_op | source)
XLA Modules:
  0.0 92.4 jit_solution(1895896976880183983)
XLA Ops:
  7.2 0.0 all-gather.2.cloned.1.call-start
  7.2 0.7 all-gather.2.cloned.1.call-update
  7.9 1.2 %dynamic-slice = u32[1]{0:T(128)} dynamic-slice(u32[32]{0:T(128)} %constant.15, u32[]{:T(128)S(6)} %add.32), dynamic_slice_sizes={1} | dynamic-slice | bytes 12
  9.8 0.9 dynamic-update-slice
  10.7 35.4 %all-reduce = bf16[128]{0:T(256)(128)(2,1)S(1)} all-reduce(bf16[128]{0:T(256)(128)(2,1)S(1)} %dynamic-update-slice), channel_id=1, replica_groups=mesh['groups'=2,'blk'=16] {'blk'}, use_global_device_ids=true, to_apply=%add | all-reduce | flops 128 | bytes 512
  46.1 17.6 %all_gather.11 = bf16[128,64]{1,0:T(8,128)(2,1)S(1)} all-gather(bf16[8,64]{1,0:T(8,128)(2,1)} %param.4), channel_id=1, replica_groups=mesh['groups'=2,'blk'=16] {'blk'}, dimensions={0}, use_global_device_ids=true | all-gather | bytes 17408 | tf_op jit(solution)/shard_map/all_gather | solution.py:20
  63.7 1.2 %multiply_reduce_fusion.1 = f32[8]{0:T(128)S(1)} fusion(bf16[8,16384]{1,0:T(8,128)(2,1)} %param.3), kind=kLoop, calls=%fused_computation.14 | loop fusion | flops 393208 | bytes 262176 | tf_op jit(solution)/shard_map/reduce_sum | solution.py:17
  64.9 0.0 all-gather.2.cloned.1.call-done
  64.9 0.0 copy-start.2
  64.9 3.2 %multiply_reduce_fusion = f32[128]{0:T(128)S(1)} fusion(bf16[128,16384]{1,0:T(8,128)(2,1)} %all-gather.2.cloned.1.call-done), kind=kLoop, calls=%fused_computation | loop fusion | flops 6291328 | bytes 4194816 | tf_op jit(solution)/shard_map/reduce_sum | solution.py:8
  68.2 0.2 copy-done
  68.4 1.3 %convert_reduce_fusion = (f32[8]{0:T(128)S(1)}, bf16[8,128]{1,0:T(8,128)(2,1)S(1)}) fusion(f32[128]{0:T(128)S(1)} %convert_element_type.21, bf16[8,16384]{1,0:T(8,128)(2,1)S(1)} %copy-done.1, bf16[128,16384]{1,0:T(8,128)(2,1)S(1)} %copy-done, f32[128]{0:T(128)S(1)} %multiply_reduce_fusion, f32[8]{0:T(128)S(1)} %multiply_reduce_fusion.1), kind=kOutput, calls=%fused_computation.15 | convolution fusion | flops 33563640 | bytes 4459584 | tf_op jit(solution)/shard_map/dot_general | solution.py:9
  69.7 0.1 convolution_divide_fusion
  69.8 0.2 convolution_bitcast_fusion
  70.0 0.4 collective-permute-start
  70.5 0.9 collective-permute-done
  71.3 2.0 %collective-permute-start.1 = (f32[64,64]{0,1:T(8,128)S(1)}, f32[64,64]{0,1:T(8,128)S(1)}, u32[]{:S(2)}, u32[]{:S(2)}) collective-permute-start(f32[64,64]{0,1:T(8,128)S(1)} %add.28), channel_id=1, source_target_pairs={{0,2},{1,3},{2,0},{3,1},{4,6},{5,7},{6,4},{7,5},{8,10},{9,11},{10,... | collective-permute-start | bytes 49160 | tf_op jit(solution)/shard_map/ppermute | solution.py:38
  73.3 1.9 %collective-permute-done.1 = f32[64,64]{0,1:T(8,128)S(1)} collective-permute-done((f32[64,64]{0,1:T(8,128)S(1)}, f32[64,64]{0,1:T(8,128)S(1)}, u32[]{:S(2)}, u32[]{:S(2)}) %collective-permute-start.1) | collective-permute-done | bytes 16416 | tf_op jit(solution)/shard_map/ppermute | solution.py:38
  75.2 0.4 collective-permute-start.2
  75.6 3.6 %collective-permute-done.2 = f32[64,64]{0,1:T(8,128)S(1)} collective-permute-done((f32[64,64]{0,1:T(8,128)S(1)}, f32[64,64]{0,1:T(8,128)S(1)}, u32[]{:S(2)}, u32[]{:S(2)}) %collective-permute-start.2) | collective-permute-done | bytes 16416 | tf_op jit(solution)/shard_map/ppermute | solution.py:38
  79.2 0.7 collective-permute-start.3
  79.8 4.3 %collective-permute-done.3 = f32[64,64]{0,1:T(8,128)S(1)} collective-permute-done((f32[64,64]{0,1:T(8,128)S(1)}, f32[64,64]{0,1:T(8,128)S(1)}, u32[]{:S(2)}, u32[]{:S(2)}) %collective-permute-start.3) | collective-permute-done | bytes 16416 | tf_op jit(solution)/shard_map/ppermute | solution.py:38
  84.1 0.7 fusion.8
  84.9 0.7 copy.5
  (10 shorter events, 0.0 us)
Async XLA Ops:
  7.2 61.0 %copy-start.1 = (bf16[8,16384]{1,0:T(8,128)(2,1)S(1)}, bf16[8,16384]{1,0:T(8,128)(2,1)}, u32[]{:S(2)}) copy-start(bf16[8,16384]{1,0:T(8,128)(2,1)} %param.3) | copy-start | bytes 786436
  7.2 57.7 %all-gather.2.cloned.1.call-start = ((), (), s32[]{:S(2)}) async-start(), calls=%async_computation | async-start | bytes 4456448 | tf_op jit(solution)/shard_map/all_gather | solution.py:19
  64.9 3.5 %copy-start = (bf16[128,16384]{1,0:T(8,128)(2,1)S(1)}, bf16[128,16384]{1,0:T(8,128)(2,1)}, u32[]{:S(2)}) copy-start(bf16[128,16384]{1,0:T(8,128)(2,1)} %all-gather.2.cloned.1.call-done) | copy-start | bytes 12582916
  64.9 4.9 %copy-start.2 = (bf16[8,64]{1,0:T(8,128)(2,1)S(1)}, bf16[8,64]{1,0:T(8,128)(2,1)}, u32[]{:S(2)}) copy-start(bf16[8,64]{1,0:T(8,128)(2,1)} %param.4) | copy-start | bytes 3076
  70.0 1.3 %collective-permute-start = (f32[64,64]{0,1:T(8,128)S(1)}, f32[64,64]{0,1:T(8,128)S(1)}, u32[]{:S(2)}, u32[]{:S(2)}) collective-permute-start(f32[64,64]{0,1:T(8,128)S(1)} %convolution_bitcast_fusion), channel_id=1, source_target_pairs={{0,1},{1,0},{2,3},{3,2},{4,5},{5,4},{6,7},{7,6},{8,9},{9,8},{10,11... | collective-permute-start | bytes 49160 | tf_op jit(solution)/shard_map/ppermute | solution.py:38
  71.3 3.9 %collective-permute-start.1 = (f32[64,64]{0,1:T(8,128)S(1)}, f32[64,64]{0,1:T(8,128)S(1)}, u32[]{:S(2)}, u32[]{:S(2)}) collective-permute-start(f32[64,64]{0,1:T(8,128)S(1)} %add.28), channel_id=1, source_target_pairs={{0,2},{1,3},{2,0},{3,1},{4,6},{5,7},{6,4},{7,5},{8,10},{9,11},{10,... | collective-permute-start | bytes 49160 | tf_op jit(solution)/shard_map/ppermute | solution.py:38
  75.2 3.9 %collective-permute-start.2 = (f32[64,64]{0,1:T(8,128)S(1)}, f32[64,64]{0,1:T(8,128)S(1)}, u32[]{:S(2)}, u32[]{:S(2)}) collective-permute-start(f32[64,64]{0,1:T(8,128)S(1)} %add.29), channel_id=1, source_target_pairs={{0,4},{1,5},{2,6},{3,7},{4,0},{5,1},{6,2},{7,3},{8,12},{9,13},{10,... | collective-permute-start | bytes 49160 | tf_op jit(solution)/shard_map/ppermute | solution.py:38
  79.2 5.0 %collective-permute-start.3 = (f32[64,64]{0,1:T(8,128)S(1)}, f32[64,64]{0,1:T(8,128)S(1)}, u32[]{:S(2)}, u32[]{:S(2)}) collective-permute-start(f32[64,64]{0,1:T(8,128)S(1)} %add.30), channel_id=1, source_target_pairs={{0,8},{1,9},{2,10},{3,11},{4,12},{5,13},{6,14},{7,15},{8,0},{9,1},... | collective-permute-start | bytes 49160 | tf_op jit(solution)/shard_map/ppermute | solution.py:38
Sparse Core Ops, SparseCore 0:
  10.2 53.5 all-gather.1
